TPU v7x, 256 devices: a whole 4x4x8 slice. The times are simulated.
256 devices in a mesh: aux: 2 (over core), row: 8 (over z), col: 16 (over x, y).
Axes of the slice: x: 4, y: 4, z: 8, core: 2. Of those that a mesh axis runs over, the one named last changes fastest.
Arguments:
- coulomb: bfloat16 [64, 2048, 2048], P('aux', 'row', 'col'), may hold values from -6 to 6
- occupied: bfloat16 [2048, 2048], P('row'), may hold values from -0.125 to 0.125
- virtual: bfloat16 [2048, 2048], P('row'), may hold values from -0.125 to 0.125
- tile_mask: int32 [16, 16], replicated, may hold values 0 or 1
Outputs:
- chi: float32 [64, 64], P('aux')
All inputs are finite; a program needn't handle non-finite values.
Results may differ from a plain program's by a relative error of at most 0.0042.
Values may be sent and summed in bfloat16 or wider, within the bound.
A program may use at most 128 MiB of HBM per device.

v0:
```python
import jax
import jax.numpy as jnp
from jax import lax
from jax.sharding import PartitionSpec as P

NAO = 2048
TILE = 128


def swapped(value, axis, apart):
    mask = 2**apart
    pairs = [(source, source ^ mask) for source in range(lax.axis_size(axis))]
    return lax.ppermute(value, axis, pairs)


def spread_density(local):
    cols = lax.axis_size("col")
    cores = lax.axis_size("aux")
    width = local.shape[1] // cols
    piece = lax.dynamic_slice_in_dim(local, lax.axis_index("col") * width, width, axis=1)
    column = lax.all_gather(piece, "row", axis=0, tiled=True)
    height = column.shape[0] // cores
    part = lax.dynamic_slice_in_dim(column, lax.axis_index("aux") * height, height, axis=0)
    rows = lax.all_gather(part, "col", axis=1, tiled=True)
    return lax.all_gather(rows, "aux", axis=0, tiled=True)


def shards(coulomb, occupied, virtual, tile_mask):
    rows = lax.axis_size("row")
    cols = lax.axis_size("col")
    pdev, mrow, ncol = coulomb.shape
    nao = mrow * rows
    row_idx = lax.axis_index("row")
    col_idx = lax.axis_index("col")
    aux_idx = lax.axis_index("aux")
    tiles_r = mrow // TILE
    tiles_c = ncol // TILE
    local_tiles = lax.dynamic_slice(
        tile_mask, (row_idx * tiles_r, col_idx * tiles_c), (tiles_r, tiles_c)
    )
    local_mask = jnp.repeat(jnp.repeat(local_tiles, TILE, axis=0), TILE, axis=1).astype(
        jnp.bfloat16
    )
    screened = coulomb * local_mask[None]
    moved = lax.all_to_all(screened, "row", split_axis=0, concat_axis=1, tiled=True)
    pieces = moved.shape[0]
    occ_all, virt_all = (spread_density(occupied), spread_density(virtual))
    half = jnp.einsum("ml,pmn->pln", occ_all, moved, preferred_element_type=jnp.float32).astype(
        jnp.bfloat16
    )
    jpart = mrow // cols
    shaped = half.reshape(pieces, rows, cols, jpart, ncol)
    spread = lax.all_to_all(shaped, "col", split_axis=2, concat_axis=4, tiled=True)
    spread = spread.reshape(pieces, rows * jpart, nao)
    dressed = jnp.einsum(
        "pln,ns->pls", spread, virt_all, preferred_element_type=jnp.float32
    ).astype(jnp.bfloat16)
    layered = dressed.reshape(pieces, rows, 1, jpart, cols, ncol)
    returned = lax.all_to_all(
        lax.all_to_all(layered, "row", split_axis=1, concat_axis=0, tiled=True),
        "col",
        split_axis=4,
        concat_axis=2,
        tiled=True,
    )
    aligned = returned.reshape(pdev, mrow, ncol)
    theirs = swapped(screened, "aux", 0)
    with_mine = jnp.einsum("pls,qls->pq", aligned, screened, preferred_element_type=jnp.float32)
    with_theirs = jnp.einsum("pls,qls->pq", aligned, theirs, preferred_element_type=jnp.float32)
    first_half = jnp.where(aux_idx == 0, with_mine, with_theirs)
    second_half = jnp.where(aux_idx == 0, with_theirs, with_mine)
    partial_chi = jnp.concatenate([first_half, second_half], axis=1)
    slots = lax.axis_size("aux")
    placed = jnp.zeros((slots,) + partial_chi.shape, partial_chi.dtype)
    placed = lax.dynamic_update_index_in_dim(placed, partial_chi, aux_idx, 0)
    total = lax.psum(placed, ("aux", "row", "col"))
    total_chi = lax.dynamic_index_in_dim(total, aux_idx, 0, keepdims=False)
    return total_chi / NAO


def solution(mesh):
    placed = (P("aux", "row", "col"), P("row", None), P("row", None), P())
    return jax.shard_map(
        shards, mesh=mesh, in_specs=placed, out_specs=P("aux", None), check_vma=False
    )
```

profile of v0, /device:TPU:1, one launch (start us, length us, event | category | flops | bytes accessed | tf_op | source)
XLA Modules:
  0.0 467.8 jit_solution(12967270680666020211)
XLA Ops:
  6.5 1.2 copy-done
  7.8 23.7 %all_gather.18 = bf16[2048,128]{1,0:T(8,128)(2,1)S(1)} all-gather(bf16[256,128]{1,0:T(8,128)(2,1)S(1)} %constant_dynamic-slice_fusion.3), channel_id=1, replica_groups=mesh['aux'=2,'row'=8,'col'=16] {'row'}, dimensions={0}, use_global_device_ids=true | all-gather | bytes 589824 | tf_op jit(solution)/shard_map/all_gather | solution.py:21
  33.2 19.8 %all_gather.21 = bf16[2048,128]{1,0:T(8,128)(2,1)S(1)} all-gather(bf16[256,128]{1,0:T(8,128)(2,1)S(1)} %constant_dynamic-slice_fusion.1), channel_id=1, replica_groups=mesh['aux'=2,'row'=8,'col'=16] {'row'}, dimensions={0}, use_global_device_ids=true | all-gather | bytes 589824 | tf_op jit(solution)/shard_map/all_gather | solution.py:21
  53.8 45.8 %all-gather.5.cloned.1.call-done = bf16[1024,2048]{1,0:T(8,128)(2,1)} async-done(((bf16[1024,128]{1,0:T(8,128)(2,1)}), bf16[1024,2048]{1,0:T(8,128)(2,1)}) %all-gather.5.cloned.1.call-update) | async-done | bytes 4194320 | tf_op jit(solution)/shard_map/all_gather | solution.py:24
  99.6 64.4 %all-gather.9.cloned.1.call-done = bf16[1024,2048]{1,0:T(8,128)(2,1)} async-done(((bf16[1024,128]{1,0:T(8,128)(2,1)}), bf16[1024,2048]{1,0:T(8,128)(2,1)}) %all-gather.9.cloned.1.call-update) | async-done | bytes 4194320 | tf_op jit(solution)/shard_map/all_gather | solution.py:24
  165.0 2.8 copy_multiply_fusion
  168.6 55.1 %all_to_all.66 = bf16[32,256,128]{2,1,0:T(8,128)(2,1)} all-to-all(bf16[32,256,128]{2,1,0:T(8,128)(2,1)S(1)} %copy.15), channel_id=1, replica_groups=mesh['aux'=2,'row'=8,'col'=16] {'row'}, dimensions={0} | all-to-all | bytes 4194304 | tf_op jit(solution)/shard_map/all_to_all | solution.py:45
  223.7 4.5 copy.16
  228.2 4.2 all_to_all.51
  232.4 9.8 %fusion.10 = bf16[4,2048,128]{1,2,0:T(8,128)(2,1)} fusion(bf16[4,2048,128]{1,2,0:T(8,128)(2,1)} %all_to_all.51, bf16[2048,2048]{1,0:T(8,128)(2,1)} %all-gather.7.cloned.1.call-done), kind=kOutput, calls=%fused_computation.6 | convolution fusion | flops 4296015872 | bytes 12582912 | tf_op jit(solution)/shard_map/ml,pmn->pln/dot_general | solution.py:48
  242.3 3.9 copy.17
  246.2 2.2 copy.18
  248.4 28.7 %all_to_all.67 = bf16[4,8,16,16,128]{4,3,1,0,2:T(8,128)(2,1)S(1)} all-to-all(bf16[4,8,16,16,128]{4,3,1,0,2:T(8,128)(2,1)S(1)} %copy.18), channel_id=1, replica_groups=mesh['aux'=2,'row'=8,'col'=16] {'col'}, dimensions={2} | all-to-all | bytes 4194304 | tf_op jit(solution)/shard_map/all_to_all | solution.py:53
  277.1 3.8 copy.19
  280.8 4.2 reshape.37
  285.0 8.5 %fusion.7 = bf16[4,128,2048]{2,1,0:T(8,128)(2,1)S(1)} fusion(bf16[4,128,2048]{2,1,0:T(8,128)(2,1)} %reshape.37, bf16[2048,2048]{1,0:T(8,128)(2,1)} %all-gather.11.cloned.1.call-done), kind=kOutput, calls=%fused_computation.5 | convolution fusion | flops 4296015872 | bytes 12582912 | tf_op jit(solution)/shard_map/pln,ns->pls/dot_general | solution.py:55
  294.8 51.9 %all_to_all.68 = bf16[4,8,1,16,16,128]{5,4,3,0,2,1:T(8,128)(2,1)S(1)} all-to-all(bf16[4,8,1,16,16,128]{5,4,3,0,2,1:T(8,128)(2,1)S(1)} %copy.20), channel_id=1, replica_groups=mesh['aux'=2,'row'=8,'col'=16] {'row'}, dimensions={1} | all-to-all | bytes 4194304 | tf_op jit(solution)/shard_map/all_to_all | solution.py:60
  346.6 1.9 copy.21
  348.5 5.3 %all-to-all-start.3 = ((bf16[32,1,1,16,16,128]{5,3,0,2,1,4:T(8,128)(2,1)}), bf16[32,1,1,16,16,128]{5,3,0,2,1,4:T(8,128)(2,1)}, u32[]{:S(2)}, u32[]{:S(2)}) async-start(bf16[32,1,1,16,16,128]{5,3,0,2,1,4:T(8,128)(2,1)} %copy.21), calls=%async_computation.3 | async-start | bytes 4194304 | tf_op jit(solution)/shard_map/all_to_all | solution.py:59
  353.8 4.7 collective-permute-start
  358.5 19.6 %all-to-all-done.3 = bf16[32,1,1,16,16,128]{5,3,0,2,1,4:T(8,128)(2,1)} async-done(((bf16[32,1,1,16,16,128]{5,3,0,2,1,4:T(8,128)(2,1)}), bf16[32,1,1,16,16,128]{5,3,0,2,1,4:T(8,128)(2,1)}, u32[]{:S(2)}, u32[]{:S(2)}) %all-to-all-start.3) | async-done | bytes 2097184 | tf_op jit(solution)/shard_map/all_to_all | solution.py:59
  378.0 2.1 copy.22
  380.9 2.3 broadcast_select_fusion.1
  383.3 77.4 %psum.7 = f32[2,32,64]{2,1,0:T(8,128)S(1)} all-reduce(f32[2,32,64]{2,1,0:T(8,128)S(1)} %fusion.13), channel_id=1, replica_groups=mesh['aux'=2,'row'=8,'col'=16] {'aux','row','col'}, use_global_device_ids=true, to_apply=%region_0.1 | all-reduce | flops 4096 | bytes 32768 | tf_op jit(solution)/shard_map/psum | solution.py:76
  (27 shorter events, 6.9 us)
Async XLA Ops:
  6.5 1.2 copy-start
  6.5 93.0 %all-gather.5.cloned.1.call-start = ((), (), s32[]{:S(2)}) async-start(), calls=%async_computation.4 | async-start | bytes 4456448 | tf_op jit(solution)/shard_map/all_gather | solution.py:24
  32.3 131.7 %all-gather.9.cloned.1.call-start = ((), (), s32[]{:S(2)}) async-start(), calls=%async_computation.6 | async-start | bytes 4456448 | tf_op jit(solution)/shard_map/all_gather | solution.py:24
  53.7 178.7 %all-gather.7.cloned.1.call-start = ((), (), s32[]{:S(2)}) async-start(), calls=%async_computation.5 | async-start | bytes 12582912 | tf_op jit(solution)/shard_map/all_gather | solution.py:25
  99.6 185.5 %all-gather.11.cloned.1.call-start = ((), (), s32[]{:S(2)}) async-start(), calls=%async_computation.7 | async-start | bytes 12582912 | tf_op jit(solution)/shard_map/all_gather | solution.py:25
  348.5 29.5 %all-to-all-start.3 = ((bf16[32,1,1,16,16,128]{5,3,0,2,1,4:T(8,128)(2,1)}), bf16[32,1,1,16,16,128]{5,3,0,2,1,4:T(8,128)(2,1)}, u32[]{:S(2)}, u32[]{:S(2)}) async-start(bf16[32,1,1,16,16,128]{5,3,0,2,1,4:T(8,128)(2,1)} %copy.21), calls=%async_computation.3 | async-start | bytes 4194304 | tf_op jit(solution)/shard_map/all_to_all | solution.py:59
  353.8 27.0 %collective-permute-start = (bf16[32,256,128]{2,0,1:T(8,128)(2,1)S(1)}, bf16[32,256,128]{2,0,1:T(8,128)(2,1)}, u32[]{:S(2)}, u32[]{:S(2)}) collective-permute-start(bf16[32,256,128]{2,0,1:T(8,128)(2,1)S(1)} %copy_multiply_fusion), channel_id=1, source_target_pairs={{0,128},{128,0},{1,129},{129,1},{2,130},{130,2},{3,131},{131,3},{4... | collective-permute-start | bytes 6291464 | tf_op jit(solution)/shard_map/ppermute | solution.py:13
  380.2 81.1 %copy-start.1 = (bf16[256,2048]{1,0:T(8,128)(2,1)S(1)}, bf16[256,2048]{1,0:T(8,128)(2,1)}, u32[]{:S(2)}) copy-start(bf16[256,2048]{1,0:T(8,128)(2,1)} %param.5) | copy-start | bytes 3145732
Sparse Core Ops, SparseCore 0:
  32.4 67.0 all-gather.4
  101.9 62.0 all-gather.8
  165.8 26.2 all-gather.6
  193.7 26.4 all-gather.10
where the time goes:
time: 469 us; the launch traced here: 468 us
  blocking collectives  257 us (55%)
  waiting for transfers between devices  130 us (28%)
  local copies, waits for them, and re-layouts  32.5 us (7%)
  matrix products  21.3 us (5%)
  between operations  13.2 us (3%)
  starting transfers between devices  10.1 us (2%)
    all_gather x2, waiting for transfers between devices, spread_density(): rows = lax.all_gather(part, 'col', axis=1, tiled=True)  110 us
    psum x1, blocking collectives, shards(): total = lax.psum(placed, ('aux', 'row', 'col'))  77.4 us
    all_to_all x1, blocking collectives, shards(): lax.all_to_all(screened, 'row', split_axis=0, concat_axis=1, tiled=True)  55.1 us
    all_to_all x1, blocking collectives, shards(): lax.all_to_all(layered, 'row', split_axis=1, concat_axis=0, tiled=True)  51.9 us
    all_gather x2, blocking collectives, spread_density(): column = lax.all_gather(piece, 'row', axis=0, tiled=True)  43.5 us
    all_to_all x1, blocking collectives, shards(): lax.all_to_all(shaped, 'col', split_axis=2, concat_axis=4, tiled=True)  28.7 us
    all_to_all x1, waiting for transfers between devices, shards(): lax.all_to_all(lax.all_to_all(layered, 'row', split_axis=1, concat_axis=0...  19.6 us
    dot_general x1, matrix products, shards(): jnp.einsum('ml,pmn->pln', occ_all, moved, preferred_element_type=jnp.floa...  9.83 us
  transfers between devices with their start and end apart: 6, of which 3 were waited for; matrix products, arithmetic and copies ran while one was open for 8% of the time, Pallas kernels for 0%

commit v1 on v0

--- a/solution.py
+++ b/solution.py
@@ -5,6 +5,13 @@
 
 NAO = 2048
 TILE = 128
+
+
+def all_by_exchange(array, axis, along):
+    count = lax.axis_size(axis)
+    blocks = jnp.stack([array for _ in range(count)])
+    blocks = lax.all_to_all(blocks, axis, split_axis=0, concat_axis=0)
+    return jnp.concatenate(blocks, axis=along)
 
 
 def swapped(value, axis, apart):
@@ -22,7 +29,7 @@
     height = column.shape[0] // cores
     part = lax.dynamic_slice_in_dim(column, lax.axis_index("aux") * height, height, axis=0)
     rows = lax.all_gather(part, "col", axis=1, tiled=True)
-    return lax.all_gather(rows, "aux", axis=0, tiled=True)
+    return all_by_exchange(rows, "aux", 0)
 
 
 def shards(coulomb, occupied, virtual, tile_mask):

time: 469 us -> 402 us (0.86)
  waiting for transfers between devices: 130 us -> 49.1 us
  blocking collectives: 257 us -> 240 us
  starting transfers between devices: 10.1 us -> 26.4 us
  other arithmetic: 4.33 us -> 19.2 us
    all_gather x2, waiting for transfers between devices: 110 us -> 0.95 us  [spread_density(): rows = lax.all_gather(part, 'col', axis=1, tiled=True)]
    all_to_all x0 -> x2, waiting for transfers between devices: none -> 20.9 us  [the longest x1 20.9 us: shards(): lax.all_to_all(shaped, 'col', split_axis=2, concat_axis=4, tiled=True)]
    all_to_all x0 -> x2, starting transfers between devices: none -> 16.3 us  [the longest x1 9.52 us: all_by_exchange(): blocks = lax.all_to_all(blocks, axis, split_axis=0, concat_axis=0)]
    another operation x0 -> x2, other arithmetic: none -> 14.9 us  [all_by_exchange(): blocks = jnp.stack([array for _ in range(count)])]
    all_to_all x1, blocking collectives: 55.1 us -> 42.7 us  [shards(): lax.all_to_all(screened, 'row', split_axis=0, concat_axis=1, tiled=True)]
    all_to_all x1, waiting for transfers between devices: 19.6 us -> 27.3 us  [shards(): lax.all_to_all(lax.all_to_all(layered, 'row', split_axis=1, concat_axis=0...]
  transfers between devices with their start and end apart: 6 -> 6, of which waited for: 3 -> 3; matrix products, arithmetic and copies ran while one was open for 8% -> 13% of each run, Pallas kernels for 0% -> 0%
where the time goes in v1:
time: 402 us; the launch traced here: 401 us
  blocking collectives  240 us (60%)
  waiting for transfers between devices  49.1 us (12%)
  local copies, waits for them, and re-layouts  35.3 us (9%)
  starting transfers between devices  26.4 us (7%)
  other arithmetic  19.2 us (5%)
  matrix products  17.3 us (4%)
  between operations  13.5 us (3%)
    psum x1, blocking collectives, shards(): total = lax.psum(placed, ('aux', 'row', 'col'))  73.9 us
    all_to_all x1, blocking collectives, shards(): lax.all_to_all(layered, 'row', split_axis=1, concat_axis=0, tiled=True)  54.2 us
    all_gather x2, blocking collectives, spread_density(): column = lax.all_gather(piece, 'row', axis=0, tiled=True)  43.5 us
    all_to_all x1, blocking collectives, shards(): lax.all_to_all(screened, 'row', split_axis=0, concat_axis=1, tiled=True)  42.7 us
    all_to_all x1, waiting for transfers between devices, shards(): lax.all_to_all(lax.all_to_all(layered, 'row', split_axis=1, concat_axis=0...  27.3 us
    all_to_all x1, blocking collectives, all_by_exchange(): blocks = lax.all_to_all(blocks, axis, split_axis=0, concat_axis=0)  25.9 us
    all_to_all x1, waiting for transfers between devices, shards(): lax.all_to_all(shaped, 'col', split_axis=2, concat_axis=4, tiled=True)  20.9 us
    another operation x2, other arithmetic, all_by_exchange(): blocks = jnp.stack([array for _ in range(count)])  14.9 us
  transfers between devices with their start and end apart: 6, of which 3 were waited for; matrix products, arithmetic and copies ran while one was open for 13% of the time, Pallas kernels for 0%

profile of v1, /device:TPU:1, one launch (start us, length us, event | category | flops | bytes accessed | tf_op | source)
XLA Modules:
  0.0 401.1 jit_solution(16841177090500621050)
XLA Ops:
  7.8 23.7 %all_gather.12 = bf16[2048,128]{1,0:T(8,128)(2,1)S(1)} all-gather(bf16[256,128]{1,0:T(8,128)(2,1)S(1)} %constant_dynamic-slice_fusion.3), channel_id=1, replica_groups=mesh['aux'=2,'row'=8,'col'=16] {'row'}, dimensions={0}, use_global_device_ids=true | all-gather | bytes 589824 | tf_op jit(solution)/shard_map/all_gather | solution.py:28
  33.2 19.8 %all_gather.14 = bf16[2048,128]{1,0:T(8,128)(2,1)S(1)} all-gather(bf16[256,128]{1,0:T(8,128)(2,1)S(1)} %constant_dynamic-slice_fusion.1), channel_id=1, replica_groups=mesh['aux'=2,'row'=8,'col'=16] {'row'}, dimensions={0}, use_global_device_ids=true | all-gather | bytes 589824 | tf_op jit(solution)/shard_map/all_gather | solution.py:28
  54.7 2.8 copy_multiply_fusion
  58.3 42.7 %all_to_all.76 = bf16[32,256,128]{2,1,0:T(8,128)(2,1)} all-to-all(bf16[32,256,128]{2,1,0:T(8,128)(2,1)S(1)} %copy.15), channel_id=1, replica_groups=mesh['aux'=2,'row'=8,'col'=16] {'row'}, dimensions={0} | all-to-all | bytes 4194304 | tf_op jit(solution)/shard_map/all_to_all | solution.py:52
  101.0 4.5 %copy.16 = bf16[8,4,256,128]{2,0,3,1:T(8,128)(2,1)} copy(bf16[8,4,256,128]{3,2,1,0:T(8,128)(2,1)} %bitcast.61) | data formatting | bytes 4194304 | tf_op jit(solution)/shard_map/all_to_all | solution.py:52
  105.5 4.2 %all_to_all.57 = bf16[4,2048,128]{1,2,0:T(8,128)(2,1)} reshape(bf16[4,8,256,128]{2,1,3,0:T(8,128)(2,1)} %bitcast.62) | data formatting | bytes 4194304 | tf_op jit(solution)/shard_map/all_to_all | solution.py:52
  109.7 7.4 %pad_maximum_fusion = bf16[2,1024,2048]{2,1,0:T(8,128)(2,1)} fusion(bf16[1,1024,2048]{2,1,0:T(8,128)(2,1)} %bitcast.67), kind=kLoop, calls=%fused_computation | loop fusion | flops 4194304 | bytes 12582912 | tf_op jit(solution)/shard_map/stack | solution.py:12
  117.1 25.9 %all_to_all.77 = bf16[2,1024,2048]{2,1,0:T(8,128)(2,1)S(1)} all-to-all(bf16[2,1024,2048]{2,1,0:T(8,128)(2,1)} %pad_maximum_fusion), channel_id=1, replica_groups=mesh['aux'=2,'row'=8,'col'=16] {'aux'}, dimensions={0} | all-to-all | bytes 16777216 | tf_op jit(solution)/shard_map/all_to_all | solution.py:13
  143.0 5.8 %fusion = bf16[4,2048,128]{1,2,0:T(8,128)(2,1)} fusion(bf16[4,2048,128]{1,2,0:T(8,128)(2,1)S(1)} %copy-done.2, bf16[2048,2048,1]{1,0,2:T(8,128)(2,1)S(1)} %bitcast.60), kind=kOutput, calls=%fused_computation.4 | convolution fusion | flops 4296015872 | bytes 12582912 | tf_op jit(solution)/shard_map/ml,pmn->pln/dot_general | solution.py:55
  148.8 4.0 copy.17
  152.8 3.5 copy.18
  156.3 6.8 %all-to-all-start.2 = ((bf16[4,8,16,16,128]{4,3,1,0,2:T(8,128)(2,1)}), bf16[4,8,16,16,128]{4,3,1,0,2:T(8,128)(2,1)}, u32[]{:S(2)}, u32[]{:S(2)}) async-start(bf16[4,8,16,16,128]{4,3,1,0,2:T(8,128)(2,1)} %copy.18), calls=%async_computation.2 | async-start | bytes 4194304 | tf_op jit(solution)/shard_map/all_to_all | solution.py:60
  164.0 7.4 %pad_maximum_fusion.1 = bf16[2,1024,2048]{2,1,0:T(8,128)(2,1)} fusion(bf16[1,1024,2048]{2,1,0:T(8,128)(2,1)} %bitcast.66), kind=kLoop, calls=%fused_computation.1 | loop fusion | flops 4194304 | bytes 12582912 | tf_op jit(solution)/shard_map/stack | solution.py:12
  171.4 20.9 %all-to-all-done.2 = bf16[4,8,16,16,128]{4,3,1,0,2:T(8,128)(2,1)} async-done(((bf16[4,8,16,16,128]{4,3,1,0,2:T(8,128)(2,1)}), bf16[4,8,16,16,128]{4,3,1,0,2:T(8,128)(2,1)}, u32[]{:S(2)}, u32[]{:S(2)}) %all-to-all-start.2) | async-done | bytes 2097184 | tf_op jit(solution)/shard_map/all_to_all | solution.py:60
  192.3 9.5 %all-to-all-start.3 = ((bf16[2,1024,2048]{2,1,0:T(8,128)(2,1)}), bf16[2,1024,2048]{2,1,0:T(8,128)(2,1)}, u32[]{:S(2)}, u32[]{:S(2)}) async-start(bf16[2,1024,2048]{2,1,0:T(8,128)(2,1)} %pad_maximum_fusion.1), calls=%async_computation.3 | async-start | bytes 16777216 | tf_op jit(solution)/shard_map/all_to_all | solution.py:13
  201.8 5.3 %copy.19 = bf16[4,8,1,16,16,128]{5,4,3,1,0,2:T(8,128)(2,1)} copy(bf16[4,8,1,16,16,128]{5,3,1,0,4,2:T(8,128)(2,1)} %bitcast.9) | data formatting | bytes 4194304 | tf_op jit(solution)/shard_map/all_to_all | solution.py:60
  207.2 4.1 %reshape.44 = bf16[4,128,2048]{2,1,0:T(8,128)(2,1)} reshape(bf16[4,8,1,16,16,128]{5,4,3,1,0,2:T(8,128)(2,1)} %copy.19) | data formatting | bytes 4194304 | tf_op jit(solution)/shard_map/reshape | solution.py:61
  211.3 8.5 %convolution_convert_fusion = bf16[4,128,2048]{2,1,0:T(8,128)(2,1)S(1)} fusion(bf16[4,128,2048]{2,1,0:T(8,128)(2,1)} %reshape.44, bf16[2048,2048,1]{1,0,2:T(8,128)(2,1)} %bitcast.12), kind=kOutput, calls=%fused_computation.2 | convolution fusion | flops 4296015872 | bytes 12582912 | tf_op jit(solution)/shard_map/pln,ns->pls/dot_general | solution.py:62
  221.1 54.2 %all_to_all.78 = bf16[4,8,1,16,16,128]{5,4,3,0,2,1:T(8,128)(2,1)S(1)} all-to-all(bf16[4,8,1,16,16,128]{5,4,3,0,2,1:T(8,128)(2,1)S(1)} %copy.20), channel_id=1, replica_groups=mesh['aux'=2,'row'=8,'col'=16] {'row'}, dimensions={1} | all-to-all | bytes 4194304 | tf_op jit(solution)/shard_map/all_to_all | solution.py:67
  277.2 9.1 %all-to-all-start.5 = ((bf16[32,1,1,16,16,128]{5,3,0,2,1,4:T(8,128)(2,1)}), bf16[32,1,1,16,16,128]{5,3,0,2,1,4:T(8,128)(2,1)}, u32[]{:S(2)}, u32[]{:S(2)}) async-start(bf16[32,1,1,16,16,128]{5,3,0,2,1,4:T(8,128)(2,1)} %copy.21), calls=%async_computation.5 | async-start | bytes 4194304 | tf_op jit(solution)/shard_map/all_to_all | solution.py:66
  287.3 27.3 %all-to-all-done.5 = bf16[32,1,1,16,16,128]{5,3,0,2,1,4:T(8,128)(2,1)} async-done(((bf16[32,1,1,16,16,128]{5,3,0,2,1,4:T(8,128)(2,1)}), bf16[32,1,1,16,16,128]{5,3,0,2,1,4:T(8,128)(2,1)}, u32[]{:S(2)}, u32[]{:S(2)}) %all-to-all-start.5) | async-done | bytes 2097184 | tf_op jit(solution)/shard_map/all_to_all | solution.py:66
  314.6 2.1 copy.22
  317.4 2.3 broadcast_select_fusion.1
  319.8 73.9 %psum.7 = f32[2,32,64]{2,1,0:T(8,128)S(1)} all-reduce(f32[2,32,64]{2,1,0:T(8,128)S(1)} %fusion.1), channel_id=1, replica_groups=mesh['aux'=2,'row'=8,'col'=16] {'aux','row','col'}, use_global_device_ids=true, to_apply=%region_0.1 | all-reduce | flops 4096 | bytes 32768 | tf_op jit(solution)/shard_map/psum | solution.py:83
  (29 shorter events, 11.7 us)
Async XLA Ops:
  6.5 1.2 copy-start
  6.5 103.1 %all-gather.3.cloned.1.call-start = ((), (), s32[]{:S(2)}) async-start(), calls=%async_computation.6 | async-start | bytes 4456448 | tf_op jit(solution)/shard_map/all_gather | solution.py:31
  32.3 131.7 %all-gather.5.cloned.1.call-start = ((), (), s32[]{:S(2)}) async-start(), calls=%async_computation.7 | async-start | bytes 4456448 | tf_op jit(solution)/shard_map/all_gather | solution.py:31
  117.1 25.9 %copy-start.2 = (bf16[4,2048,128]{1,2,0:T(8,128)(2,1)S(1)}, bf16[4,2048,128]{1,2,0:T(8,128)(2,1)}, u32[]{:S(2)}) copy-start(bf16[4,2048,128]{1,2,0:T(8,128)(2,1)} %all_to_all.57) | copy-start | bytes 6291460
  156.3 36.0 %all-to-all-start.2 = ((bf16[4,8,16,16,128]{4,3,1,0,2:T(8,128)(2,1)}), bf16[4,8,16,16,128]{4,3,1,0,2:T(8,128)(2,1)}, u32[]{:S(2)}, u32[]{:S(2)}) async-start(bf16[4,8,16,16,128]{4,3,1,0,2:T(8,128)(2,1)} %copy.18), calls=%async_computation.2 | async-start | bytes 4194304 | tf_op jit(solution)/shard_map/all_to_all | solution.py:60
  192.3 19.0 %all-to-all-start.3 = ((bf16[2,1024,2048]{2,1,0:T(8,128)(2,1)}), bf16[2,1024,2048]{2,1,0:T(8,128)(2,1)}, u32[]{:S(2)}, u32[]{:S(2)}) async-start(bf16[2,1024,2048]{2,1,0:T(8,128)(2,1)} %pad_maximum_fusion.1), calls=%async_computation.3 | async-start | bytes 16777216 | tf_op jit(solution)/shard_map/all_to_all | solution.py:13
  277.2 37.4 %all-to-all-start.5 = ((bf16[32,1,1,16,16,128]{5,3,0,2,1,4:T(8,128)(2,1)}), bf16[32,1,1,16,16,128]{5,3,0,2,1,4:T(8,128)(2,1)}, u32[]{:S(2)}, u32[]{:S(2)}) async-start(bf16[32,1,1,16,16,128]{5,3,0,2,1,4:T(8,128)(2,1)} %copy.21), calls=%async_computation.5 | async-start | bytes 4194304 | tf_op jit(solution)/shard_map/all_to_all | solution.py:66
  286.3 31.1 %collective-permute-start = (bf16[32,256,128]{2,0,1:T(8,128)(2,1)S(1)}, bf16[32,256,128]{2,0,1:T(8,128)(2,1)}, u32[]{:S(2)}, u32[]{:S(2)}) collective-permute-start(bf16[32,256,128]{2,0,1:T(8,128)(2,1)S(1)} %copy_multiply_fusion), channel_id=1, source_target_pairs={{0,128},{128,0},{1,129},{129,1},{2,130},{130,2},{3,131},{131,3},{4... | collective-permute-start | bytes 6291464 | tf_op jit(solution)/shard_map/ppermute | solution.py:20
  316.7 77.6 %copy-start.1 = (bf16[256,2048]{1,0:T(8,128)(2,1)S(1)}, bf16[256,2048]{1,0:T(8,128)(2,1)}, u32[]{:S(2)}) copy-start(bf16[256,2048]{1,0:T(8,128)(2,1)} %param.5) | copy-start | bytes 3145732
Sparse Core Ops, SparseCore 0:
  32.4 67.0 all-gather.2
  101.9 62.0 all-gather.4
